TPU v7x, 32 devices: a whole 2x2x4 slice. The times are simulated.
32 devices in a mesh: dp: 16 (over z, y, x), tensor: 2 (over core).
Axes of the slice: x: 2, y: 2, z: 4, core: 2. Of those that a mesh axis runs over, the one named last changes fastest.
Arguments:
- tokens: bfloat16 [16384, 768], P('dp'), may hold values from -6 to 6
- token_slot: int32 [16, 1024], P('dp'), may hold values from 0 to 1023, each once within a row
- seq_lengths: int32 [16, 4], P('dp'), may hold values from 1 to 512, 1024 in all within a row
- query_weight: bfloat16 [768, 768], P(None, 'tensor'), may hold values from -0.3125 to 0.3125
- query_bias: float32 [768], P('tensor'), may hold values from -3 to 3
- key_weight: bfloat16 [768, 768], P(None, 'tensor'), may hold values from -0.3125 to 0.3125
- value_weight: bfloat16 [768, 768], P(None, 'tensor'), may hold values from -0.21875 to 0.21875
- value_bias: float32 [768], P('tensor'), may hold values from -3 to 3
- out_weight: bfloat16 [768, 768], P('tensor'), may hold values from -1.25 to 1.25
- out_bias: float32 [768], replicated, may hold values from -3 to 3
- first_gain: float32 [768], replicated, may hold values from 0.25 to 1.75
- first_shift: float32 [768], replicated, may hold values from -3 to 3
- up_weight: bfloat16 [768, 3072], P(None, 'tensor'), may hold values from -0.21875 to 0.21875
- up_bias: float32 [3072], P('tensor'), may hold values from -3 to 3
- down_weight: bfloat16 [3072, 768], P('tensor'), may hold values from -0.109375 to 0.109375
- down_bias: float32 [768], replicated, may hold values from -3 to 3
- second_gain: float32 [768], replicated, may hold values from 0.25 to 1.75
- second_shift: float32 [768], replicated, may hold values from -3 to 3
- cotangent: bfloat16 [16384, 768], P('dp'), may hold values from -6 to 6
Outputs:
- layer_out: bfloat16 [16384, 768], P('dp')
- input_gradient: bfloat16 [16384, 768], P('dp')
- query_weight_gradient: float32 [768, 768], P('dp', 'tensor')
- query_bias_gradient: float32 [768], P(('dp', 'tensor'))
- key_weight_gradient: float32 [768, 768], P('dp', 'tensor')
- value_weight_gradient: float32 [768, 768], P('dp', 'tensor')
- value_bias_gradient: float32 [768], P(('dp', 'tensor'))
- out_weight_gradient: float32 [768, 768], P('tensor', 'dp')
- out_bias_gradient: float32 [768], P(('dp', 'tensor'))
- first_gain_gradient: float32 [768], P(('dp', 'tensor'))
- first_shift_gradient: float32 [768], P(('dp', 'tensor'))
- up_weight_gradient: float32 [768, 3072], P('dp', 'tensor')
- up_bias_gradient: float32 [3072], P(('dp', 'tensor'))
- down_weight_gradient: float32 [3072, 768], P('tensor', 'dp')
- down_bias_gradient: float32 [768], P(('dp', 'tensor'))
- second_gain_gradient: float32 [768], P(('dp', 'tensor'))
- second_shift_gradient: float32 [768], P(('dp', 'tensor'))
Inputs may be any that keep to these rules, and one draw needn't show every extreme that they name: `token_slot`: each row orders the 1024 rows that one group receives. `seq_lengths`: each row holds one group's 4 sequence lengths in order; they sum to 1024 and the longest is 512.
All inputs are finite; a program needn't handle non-finite values.
Results may differ from a plain program's by a relative error of at most 0.015.
The roundings to bfloat16 on the way count: a program that leaves them out, or rounds other values in their place, can miss the bound.
Values may be sent and summed in bfloat16 or wider, within the bound.
No kernel may reach another device: no remote copies, remote signals or barrier semaphores. Data moves between devices by JAX's collectives and lax.ppermute only.
A program may use at most 192 MiB of HBM per device.

v0:
```python
import jax
import jax.numpy as jnp
from jax import lax
from jax.sharding import PartitionSpec as P

HD = 64


EPSILON = 1e-12
MASKED = -1e30


def product(first_op, second_op):
    return jnp.dot(first_op, second_op, preferred_element_type=jnp.float32)


def contract_rows(first_op, second_op):
    return lax.dot_general(
        first_op, second_op, (((0,), (0,)), ((), ())), preferred_element_type=jnp.float32
    )


def contract_cols(first_op, second_op):
    return lax.dot_general(
        first_op, second_op, (((1,), (1,)), ((), ())), preferred_element_type=jnp.float32
    )


def gelu_slope(values):
    cumulative = 0.5 * (1.0 + lax.erf(values * 0.7071067811865476))
    density = jnp.exp(-0.5 * values * values) * 0.3989422804014327
    return cumulative + values * density


def norm_forward(values, gain, shift):
    centre = values - jnp.mean(values, axis=-1, keepdims=True)
    inv_scale = lax.rsqrt(jnp.mean(centre * centre, axis=-1, keepdims=True) + EPSILON)
    normed = centre * inv_scale
    return (normed * gain + shift, normed, inv_scale)


def norm_backward(upstream, normed, inv_scale, gain):
    scaled = upstream * gain
    return inv_scale * (
        scaled
        - jnp.mean(scaled, axis=-1, keepdims=True)
        - normed * jnp.mean(scaled * normed, axis=-1, keepdims=True)
    )


def my_share(values):
    share_rows = values.shape[0] // lax.axis_size("tensor")
    return lax.dynamic_slice_in_dim(values, lax.axis_index("tensor") * share_rows, share_rows, 0)


def counted_rows(values):
    return my_share(values)


def combine_heads(part_sum):
    return lax.psum(part_sum, "tensor")


def masked_scores(query_block, key_rows, segment_block, segment, score_scale):
    scores = (
        jnp.einsum("qhd,khd->hqk", query_block, key_rows, preferred_element_type=jnp.float32)
        * score_scale
    )
    return jnp.where(segment_block[None, :, None] == segment[None, None, :], scores, MASKED)


def attention_forward(query_rows, key_rows, value_rows, segment):
    row_count, head_count, head_size = query_rows.shape
    score_scale = head_size ** (-0.5)
    block_rows = min(512, row_count)
    block_count = row_count // block_rows

    def one_block(pieces):
        query_block, segment_block = pieces
        scores = masked_scores(query_block, key_rows, segment_block, segment, score_scale)
        row_peak = jnp.max(scores, axis=-1, keepdims=True)
        exp_scores = jnp.exp(scores - row_peak)
        row_total = jnp.sum(exp_scores, axis=-1, keepdims=True)
        weights = (exp_scores / row_total).astype(jnp.bfloat16)
        mixed_block = jnp.einsum(
            "hqk,khd->qhd", weights, value_rows, preferred_element_type=jnp.float32
        )
        return (mixed_block.astype(jnp.bfloat16), (row_peak + jnp.log(row_total))[..., 0])

    mixed_heads, logsum = lax.map(
        one_block,
        (
            query_rows.reshape(block_count, block_rows, head_count, head_size),
            segment.reshape(block_count, block_rows),
        ),
    )
    return (mixed_heads.reshape(row_count, head_count * head_size), logsum)


def attention_backward(query_rows, key_rows, value_rows, segment, logsum, mixed_grad):
    row_count, head_count, head_size = query_rows.shape
    score_scale = head_size ** (-0.5)
    block_rows = min(512, row_count)
    block_count = row_count // block_rows

    def one_block(totals_pair, pieces):
        key_total, value_total = totals_pair
        query_block, segment_block, logsum_block, grad_block = pieces
        scores = masked_scores(query_block, key_rows, segment_block, segment, score_scale)
        softmax_rows = jnp.exp(scores - logsum_block[..., None])
        weights = softmax_rows.astype(jnp.bfloat16)
        value_total = value_total + jnp.einsum(
            "hqk,qhd->khd", weights, grad_block, preferred_element_type=jnp.float32
        )
        pulled = jnp.einsum(
            "qhd,khd->hqk", grad_block, value_rows, preferred_element_type=jnp.float32
        )
        centred = jnp.sum(softmax_rows * pulled, axis=-1, keepdims=True)
        slopes = (softmax_rows * (pulled - centred)).astype(jnp.bfloat16)
        query_part = (
            jnp.einsum("hqk,khd->qhd", slopes, key_rows, preferred_element_type=jnp.float32)
            * score_scale
        )
        key_total = (
            key_total
            + jnp.einsum("hqk,qhd->khd", slopes, query_block, preferred_element_type=jnp.float32)
            * score_scale
        )
        return ((key_total, value_total), query_part.astype(jnp.bfloat16))

    zero_rows = jnp.zeros((row_count, head_count, head_size), jnp.float32)
    (key_total, value_total), query_grad = lax.scan(
        one_block,
        (zero_rows, zero_rows),
        (
            query_rows.reshape(block_count, block_rows, head_count, head_size),
            segment.reshape(block_count, block_rows),
            logsum,
            mixed_grad.reshape(block_count, block_rows, head_count, head_size),
        ),
    )
    flat_width = head_count * head_size
    return (
        query_grad.reshape(row_count, flat_width),
        key_total.astype(jnp.bfloat16).reshape(row_count, flat_width),
        value_total.astype(jnp.bfloat16).reshape(row_count, flat_width),
    )


def local(
    tokens,
    token_slot,
    seq_lengths,
    query_weight,
    query_bias,
    key_weight,
    value_weight,
    value_bias,
    out_weight,
    out_bias,
    first_gain,
    first_shift,
    up_weight,
    up_bias,
    down_weight,
    down_bias,
    second_gain,
    second_shift,
    cotangent,
):
    groups = lax.axis_size("dp")
    row_count, feature_count = tokens.shape
    run_rows = row_count // groups
    arrived, arrived_cot = (
        lax.all_to_all(
            tokens.reshape(groups, run_rows, feature_count),
            "dp",
            split_axis=0,
            concat_axis=0,
            tiled=True,
        ),
        lax.all_to_all(
            cotangent.reshape(groups, run_rows, feature_count),
            "dp",
            split_axis=0,
            concat_axis=0,
            tiled=True,
        ),
    )
    slot_rows = token_slot[0]
    inputs = jnp.take(arrived.reshape(row_count, feature_count), slot_rows, axis=0)
    upstream = jnp.take(arrived_cot.reshape(row_count, feature_count), slot_rows, axis=0)
    positions = jnp.arange(row_count, dtype=jnp.int32)
    ends = jnp.cumsum(seq_lengths[0])
    segment = jnp.sum((positions[:, None] >= ends[None, :]).astype(jnp.int32), axis=1)
    local_heads = query_weight.shape[1] // HD
    query_rows = (
        (product(inputs, query_weight) + query_bias)
        .astype(jnp.bfloat16)
        .reshape(row_count, local_heads, HD)
    )
    key_rows = product(inputs, key_weight).astype(jnp.bfloat16).reshape(row_count, local_heads, HD)
    value_rows = (
        (product(inputs, value_weight) + value_bias)
        .astype(jnp.bfloat16)
        .reshape(row_count, local_heads, HD)
    )
    mixed_flat, logsum = attention_forward(query_rows, key_rows, value_rows, segment)
    attended = combine_heads(product(mixed_flat, out_weight))
    first_in = inputs.astype(jnp.float32) + attended + out_bias
    hidden, first_normed, first_inv = norm_forward(first_in, first_gain, first_shift)
    hidden_low = hidden.astype(jnp.bfloat16)
    inner_sum = product(hidden_low, up_weight) + up_bias
    activated = jax.nn.gelu(inner_sum, approximate=False).astype(jnp.bfloat16)
    branch = combine_heads(product(activated, down_weight))
    second_in = hidden + branch + down_bias
    output, second_normed, second_inv = norm_forward(second_in, second_gain, second_shift)
    output_low = output.astype(jnp.bfloat16)
    upstream_rows = upstream.astype(jnp.float32)
    second_grad = norm_backward(upstream_rows, second_normed, second_inv, second_gain)
    second_gain_grad = jnp.sum(counted_rows(upstream_rows * second_normed), axis=0)
    second_shift_grad = jnp.sum(counted_rows(upstream_rows), axis=0)
    down_bias_grad = jnp.sum(counted_rows(second_grad), axis=0)
    second_low = second_grad.astype(jnp.bfloat16)
    down_weight_grad = contract_rows(activated, second_low)
    inner_grad = (contract_cols(second_low, down_weight) * gelu_slope(inner_sum)).astype(
        jnp.bfloat16
    )
    up_bias_grad = jnp.sum(inner_grad, axis=0, dtype=jnp.float32)
    up_weight_grad = contract_rows(hidden_low, inner_grad)
    hidden_grad = second_grad + combine_heads(contract_cols(inner_grad, up_weight))
    first_grad = norm_backward(hidden_grad, first_normed, first_inv, first_gain)
    first_gain_grad = jnp.sum(counted_rows(hidden_grad * first_normed), axis=0)
    first_shift_grad = jnp.sum(counted_rows(hidden_grad), axis=0)
    out_bias_grad = jnp.sum(counted_rows(first_grad), axis=0)
    first_low = first_grad.astype(jnp.bfloat16)
    out_weight_grad = contract_rows(mixed_flat, first_low)
    mixed_grad = contract_cols(first_low, out_weight).astype(jnp.bfloat16)
    query_grad, key_grad, value_grad = attention_backward(
        query_rows,
        key_rows,
        value_rows,
        segment,
        logsum,
        mixed_grad.reshape(row_count, local_heads, HD),
    )
    query_bias_grad = jnp.sum(query_grad, axis=0, dtype=jnp.float32)
    value_bias_grad = jnp.sum(value_grad, axis=0, dtype=jnp.float32)
    query_weight_grad = contract_rows(inputs, query_grad)
    key_weight_grad = contract_rows(inputs, key_grad)
    value_weight_grad = contract_rows(inputs, value_grad)
    input_part = (
        contract_cols(query_grad, query_weight)
        + contract_cols(key_grad, key_weight)
        + contract_cols(value_grad, value_weight)
    )
    input_low = (first_grad + combine_heads(input_part)).astype(jnp.bfloat16)
    inverse = jnp.zeros((row_count,), jnp.int32).at[slot_rows].set(positions)
    back_out = jnp.take(output_low, inverse, axis=0).reshape(groups, run_rows, feature_count)
    back_grad = jnp.take(input_low, inverse, axis=0).reshape(groups, run_rows, feature_count)
    layer_out, input_gradient = (
        lax.all_to_all(back_out, "dp", split_axis=0, concat_axis=0, tiled=True),
        lax.all_to_all(back_grad, "dp", split_axis=0, concat_axis=0, tiled=True),
    )
    tensor_index = lax.axis_index("tensor")

    def padded(values, full_length):
        return lax.dynamic_update_slice_in_dim(
            jnp.zeros((full_length,), jnp.float32), values, tensor_index * values.shape[0], 0
        )

    full_hidden = up_weight.shape[1] * lax.axis_size("tensor")
    (
        query_bias_sum,
        value_bias_sum,
        out_bias_sum,
        first_gain_sum,
        first_shift_sum,
        up_bias_sum,
        down_bias_sum,
        second_gain_sum,
        second_shift_sum,
    ) = (
        lax.psum_scatter(
            padded(query_bias_grad, feature_count),
            ("dp", "tensor"),
            scatter_dimension=0,
            tiled=True,
        ),
        lax.psum_scatter(
            padded(value_bias_grad, feature_count),
            ("dp", "tensor"),
            scatter_dimension=0,
            tiled=True,
        ),
        lax.psum_scatter(out_bias_grad, ("dp", "tensor"), scatter_dimension=0, tiled=True),
        lax.psum_scatter(first_gain_grad, ("dp", "tensor"), scatter_dimension=0, tiled=True),
        lax.psum_scatter(first_shift_grad, ("dp", "tensor"), scatter_dimension=0, tiled=True),
        lax.psum_scatter(
            padded(up_bias_grad, full_hidden), ("dp", "tensor"), scatter_dimension=0, tiled=True
        ),
        lax.psum_scatter(down_bias_grad, ("dp", "tensor"), scatter_dimension=0, tiled=True),
        lax.psum_scatter(second_gain_grad, ("dp", "tensor"), scatter_dimension=0, tiled=True),
        lax.psum_scatter(second_shift_grad, ("dp", "tensor"), scatter_dimension=0, tiled=True),
    )
    query_weight_sum, key_weight_sum, value_weight_sum, up_weight_sum = (
        lax.psum_scatter(query_weight_grad, "dp", scatter_dimension=0, tiled=True),
        lax.psum_scatter(key_weight_grad, "dp", scatter_dimension=0, tiled=True),
        lax.psum_scatter(value_weight_grad, "dp", scatter_dimension=0, tiled=True),
        lax.psum_scatter(up_weight_grad, "dp", scatter_dimension=0, tiled=True),
    )
    out_weight_sum, down_weight_sum = (
        lax.psum_scatter(out_weight_grad, "dp", scatter_dimension=1, tiled=True),
        lax.psum_scatter(down_weight_grad, "dp", scatter_dimension=1, tiled=True),
    )
    return (
        layer_out.reshape(row_count, feature_count),
        input_gradient.reshape(row_count, feature_count),
        query_weight_sum,
        query_bias_sum,
        key_weight_sum,
        value_weight_sum,
        value_bias_sum,
        out_weight_sum,
        out_bias_sum,
        first_gain_sum,
        first_shift_sum,
        up_weight_sum,
        up_bias_sum,
        down_weight_sum,
        down_bias_sum,
        second_gain_sum,
        second_shift_sum,
    )


def solution(mesh):
    in_specs = (
        P("dp", None),
        P("dp", None),
        P("dp", None),
        P(None, "tensor"),
        P("tensor"),
        P(None, "tensor"),
        P(None, "tensor"),
        P("tensor"),
        P("tensor", None),
        P(),
        P(),
        P(),
        P(None, "tensor"),
        P("tensor"),
        P("tensor", None),
        P(),
        P(),
        P(),
        P("dp", None),
    )
    out_specs = (
        P("dp", None),
        P("dp", None),
        P("dp", "tensor"),
        P(("dp", "tensor")),
        P("dp", "tensor"),
        P("dp", "tensor"),
        P(("dp", "tensor")),
        P("tensor", "dp"),
        P(("dp", "tensor")),
        P(("dp", "tensor")),
        P(("dp", "tensor")),
        P("dp", "tensor"),
        P(("dp", "tensor")),
        P("tensor", "dp"),
        P(("dp", "tensor")),
        P(("dp", "tensor")),
        P(("dp", "tensor")),
    )
    return jax.shard_map(local, mesh=mesh, in_specs=in_specs, out_specs=out_specs, check_vma=False)
```

profile of v0, /device:TPU:0, one launch (start us, length us, event | category | flops | bytes accessed | tf_op | source)
XLA Modules:
  0.0 1177.1 jit_solution(9783451068506743058)
XLA Ops:
  7.2 8.5 all-to-all-start
  16.1 33.8 %all-to-all-done = bf16[16,64,768]{2,1,0:T(8,128)(2,1)} async-done(((bf16[16,64,768]{2,1,0:T(8,128)(2,1)}), bf16[16,64,768]{2,1,0:T(8,128)(2,1)}, u32[]{:S(2)}, u32[]{:S(2)}) %all-to-all-start) | async-done | bytes 1572896 | tf_op jit(solution)/shard_map/all_to_all | solution.py:175
  50.0 7.2 gather_fusion
  71.0 25.5 %while.27 = (s32[]{:T(128)}, bf16[2,512,6,64]{1,3,2,0:T(8,128)(2,1)}, f32[2,6,512]{2,1,0:T(8,128)S(1)}, s32[2,512]{1,0:T(2,128)S(1)}, s32[1024]{0:T(1024)S(1)}, ...) while((s32[]{:T(128)}, ...), condition=%wide.region_5.7_spmd, body=%wide.region_2.6_spmd.sunk | while | flops 843772928 | bytes 51771592 | solution.py:90
  78.5 4.4 fusion.132
  91.2 4.4 fusion.132
  102.8 25.1 %all-reduce.15.cloned.1.call-done = f32[1024,768]{1,0:T(8,128)} async-done(((f32[1024,768]{1,0:T(8,128)}), f32[1024,768]{1,0:T(8,128)}) %all-reduce.15.cloned.1.call-update) | async-done | bytes 3145744 | tf_op jit(solution)/shard_map/psum | solution.py:61
  134.2 16.8 %fusion.39 = (bf16[1024,1536]{1,0:T(8,128)(2,1)S(1)}, f32[1024,1536]{1,0:T(8,128)}) fusion(f32[1536]{0:T(1024)S(1)} %copy-done.59, bf16[768,1536]{1,0:T(8,128)(2,1)S(1)} %copy-done, f32[1024,768]{1,0:T(8,128)S(1)} %subtract_multiply_fusion.3, f32[768]{0:T(1024)S(1)} %copy-done.44, f32[768]{0:T(1024)S(1)} %copy-done.42), kind=kOutput, calls=%fused_computation.58 | convolution fusion | flops 2522087424 | bytes 14954496 | tf_op jit(solution)/shard_map/dot_general | solution.py:14
  157.0 45.3 %all_to_all.20 = bf16[16,64,768]{2,1,0:T(8,128)(2,1)} all-to-all(bf16[16,64,768]{2,1,0:T(8,128)(2,1)} %bitcast.159), channel_id=1, replica_groups=mesh['dp'=16,'tensor'=2] {'dp'}, dimensions={0} | all-to-all | bytes 3145728 | tf_op jit(solution)/shard_map/all_to_all | solution.py:182
  202.3 7.2 gather_fusion.2
  219.6 5.3 convert_reduce_fusion
  231.0 21.7 %all-reduce.19.cloned.1.call-done = f32[1024,768]{1,0:T(8,128)} async-done(((f32[1024,768]{1,0:T(8,128)}), f32[1024,768]{1,0:T(8,128)}) %all-reduce.19.cloned.1.call-update) | async-done | bytes 3145744 | tf_op jit(solution)/shard_map/psum | solution.py:61
  267.8 53.1 %while.28 = (s32[]{:T(128)}, f32[1024,6,64]{0,2,1:T(8,128)S(1)}, f32[1024,6,64]{0,2,1:T(8,128)}, bf16[2,512,6,64]{1,3,2,0:T(8,128)(2,1)}, bf16[2,512,6,64]{1,3,2...) while((s32[]{:T(128)}, f32[1024,6,64]{0,2,1:T(8,128)S(1)}, ...), condition=%wide.region_20.22_spmd.clone, body=%wide.region_18.21_spmd.clone.sunk | while | flops 2063332352 | bytes 141789472 | solution.py:132
  271.2 4.7 bitcast_add_fusion.5
  275.9 5.4 multiply_reduce_fusion.8
  281.3 5.1 multiply_convert_fusion.2
  286.4 5.9 fusion.143
  297.1 5.8 bitcast_add_fusion.5
  302.9 5.4 multiply_reduce_fusion.8
  308.3 5.1 multiply_convert_fusion.2
  313.4 5.9 fusion.143
  344.2 8.1 fusion.60
  354.4 6.5 fusion.63
  373.1 5.2 gather_fusion.3
  381.2 47.7 %all_to_all.21 = bf16[16,64,768]{2,1,0:T(8,128)(2,1)} all-to-all(bf16[16,64,768]{2,1,0:T(8,128)(2,1)S(1)} %bitcast.149), channel_id=1, replica_groups=mesh['dp'=16,'tensor'=2] {'dp'}, dimensions={0} | all-to-all | bytes 3145728 | tf_op jit(solution)/shard_map/all_to_all | solution.py:262
  428.9 4.4 all-to-all-start.3
  444.5 47.5 %all-reduce.9 = (f32[768]{0:T(1024)S(1)}, f32[768]{0:T(1024)S(1)}, f32[768]{0:T(1024)S(1)}, f32[768]{0:T(1024)S(1)}, f32[768]{0:T(1024)S(1)}, /*index=5*/f32[307...) all-reduce(f32[768]{0:T(1024)S(1)} %dynamic_update_slice.20, ...), channel_id=3, replica_groups=mesh['dp'=16,'tensor'=2] {'dp','tensor'}, use_global_device_ids=true, to_apply=%region_24.26.clone | all-reduce | flops 9216 | bytes 73728
  497.3 127.9 %reduce-scatter.11.cloned.1.call-done = f32[48,384]{1,0:T(8,128)} async-done(((f32[768,384]{1,0:T(8,128)}), f32[48,384]{1,0:T(8,128)}) %reduce-scatter.11.cloned.1.call-update) | async-done | bytes 73744 | tf_op jit(solution)/shard_map/reduce_scatter | solution.py:309
  625.3 128.0 %reduce-scatter.9.cloned.1.call-done = f32[48,384]{1,0:T(8,128)} async-done(((f32[768,384]{1,0:T(8,128)}), f32[48,384]{1,0:T(8,128)}) %reduce-scatter.9.cloned.1.call-update) | async-done | bytes 73744 | tf_op jit(solution)/shard_map/reduce_scatter | solution.py:308
  753.2 128.0 %reduce-scatter.7.cloned.1.call-done = f32[48,384]{1,0:T(8,128)} async-done(((f32[768,384]{1,0:T(8,128)}), f32[48,384]{1,0:T(8,128)}) %reduce-scatter.7.cloned.1.call-update) | async-done | bytes 73744 | tf_op jit(solution)/shard_map/reduce_scatter | solution.py:307
  881.2 141.3 %reduce-scatter.17.cloned.1.call-done = f32[1536,48]{0,1:T(8,128)} async-done(((f32[1536,768]{0,1:T(8,128)}), f32[1536,48]{0,1:T(8,128)}) %reduce-scatter.17.cloned.1.call-update) | async-done | bytes 294928 | tf_op jit(solution)/shard_map/reduce_scatter | solution.py:314
  1022.5 142.0 %reduce-scatter.15.cloned.1.call-done = f32[48,1536]{1,0:T(8,128)} async-done(((f32[768,1536]{1,0:T(8,128)}), f32[48,1536]{1,0:T(8,128)}) %reduce-scatter.15.cloned.1.call-update) | async-done | bytes 294928 | tf_op jit(solution)/shard_map/reduce_scatter | solution.py:310
  (276 shorter events, 151.5 us)
Async XLA Ops:
  7.2 127.0 %copy-start = (bf16[768,1536]{1,0:T(8,128)(2,1)S(1)}, bf16[768,1536]{1,0:T(8,128)(2,1)}, u32[]{:S(2)}) copy-start(bf16[768,1536]{1,0:T(8,128)(2,1)} %param.37) | copy-start | bytes 7077892
  7.2 8.6 copy-start.62
  7.2 8.9 copy-start.48
  7.2 42.8 %all-to-all-start = ((bf16[16,64,768]{2,1,0:T(8,128)(2,1)}), bf16[16,64,768]{2,1,0:T(8,128)(2,1)}, u32[]{:S(2)}, u32[]{:S(2)}) async-start(bf16[16,64,768]{2,1,0:T(8,128)(2,1)} %bitcast.158), calls=%async_computation | async-start | bytes 3145728 | tf_op jit(solution)/shard_map/all_to_all | solution.py:175
  15.7 112.2 %all-reduce.15.cloned.1.call-start = ((), (), s32[]{:S(2)}) async-start(), calls=%async_computation.10 | async-start | bytes 6291456 | tf_op jit(solution)/shard_map/psum | solution.py:61
  16.1 199.9 %copy-start.46 = (pred[1024]{0:T(1024)(128)(4,1)}, pred[1024]{0:T(1024)(128)(4,1)S(1)}, u32[]{:S(2)}) copy-start(pred[1024]{0:T(1024)(128)(4,1)S(1)} %compare_and_fusion.1) | copy-start | bytes 3076
  16.1 41.1 %copy-start.51 = (s32[1024]{0:T(1024)}, s32[1024]{0:T(1024)S(1)}, u32[]{:S(2)}) copy-start(s32[1024]{0:T(1024)S(1)} %fusion.67) | copy-start | bytes 12292
  50.0 7.2 copy-start.38
  50.0 7.2 copy-start.60
  96.5 36.5 %copy-start.9 = (bf16[1024,6,64]{0,2,1:T(8,128)(2,1)}, bf16[1024,6,64]{0,2,1:T(8,128)(2,1)S(1)}, u32[]{:S(2)}) copy-start(bf16[1024,6,64]{0,2,1:T(8,128)(2,1)S(1)} %get-tuple-element.546) | copy-start | bytes 2359300
  99.8 28.1 %copy-start.50 = (f32[768]{0:T(1024)S(1)}, f32[768]{0:T(1024)}, u32[]{:S(2)}) copy-start(f32[768]{0:T(1024)} %param.34) | copy-start | bytes 9220
  102.6 106.9 %all-reduce.17.cloned.1.call-start = ((), (), s32[]{:S(2)}) async-start(), calls=%async_computation.11 | async-start | bytes 6291456 | tf_op jit(solution)/shard_map/psum | solution.py:61
  134.2 16.8 %copy-start.4 = (f32[1024,768]{1,0:T(8,128)}, f32[1024,768]{1,0:T(8,128)S(1)}, u32[]{:S(2)}) copy-start(f32[1024,768]{1,0:T(8,128)S(1)} %subtract_multiply_fusion.3) | copy-start | bytes 9437188
  134.2 18.5 %copy-start.57 = (bf16[1536,768]{1,0:T(8,128)(2,1)S(1)}, bf16[1536,768]{1,0:T(8,128)(2,1)}, u32[]{:S(2)}) copy-start(bf16[1536,768]{1,0:T(8,128)(2,1)} %param.39) | copy-start | bytes 7077892
  157.0 45.4 %copy-start.52 = (s32[1024]{0:T(1024)S(1)}, s32[1024]{0:T(1024)}, u32[]{:S(2)}) copy-start(s32[1024]{0:T(1024)} %copy-done.51) | copy-start | bytes 12292
  157.0 95.7 %all-reduce.19.cloned.1.call-start = ((), (), s32[]{:S(2)}) async-start(), calls=%async_computation.12 | async-start | bytes 6291456 | tf_op jit(solution)/shard_map/psum | solution.py:61
  202.3 7.2 copy-start.55
  218.4 6.5 copy-start.22
  230.9 21.8 %copy-start.5 = (f32[1024,768]{1,0:T(8,128)S(1)}, f32[1024,768]{1,0:T(8,128)}, u32[]{:S(2)}) copy-start(f32[1024,768]{1,0:T(8,128)} %copy-done.4) | copy-start | bytes 9437188
  231.0 139.0 %all-reduce.21.cloned.1.call-start = ((), (), s32[]{:S(2)}) async-start(), calls=%async_computation.13 | async-start | bytes 6291456 | tf_op jit(solution)/shard_map/psum | solution.py:61
  261.6 6.2 copy-start.8
  261.6 6.2 copy-start.10
  286.4 5.9 copy-start.14
  330.1 167.2 %reduce-scatter.13.cloned.1.call-start = ((), (), s32[]{:S(2)}) async-start(), calls=%async_computation.17 | async-start | bytes 1253376 | tf_op jit(solution)/shard_map/reduce_scatter | solution.py:313
  335.2 290.0 %reduce-scatter.11.cloned.1.call-start = ((), (), s32[]{:S(2)}) async-start(), calls=%async_computation.16 | async-start | bytes 1253376 | tf_op jit(solution)/shard_map/reduce_scatter | solution.py:309
  339.4 413.8 %reduce-scatter.9.cloned.1.call-start = ((), (), s32[]{:S(2)}) async-start(), calls=%async_computation.15 | async-start | bytes 1253376 | tf_op jit(solution)/shard_map/reduce_scatter | solution.py:308
  341.8 539.4 %reduce-scatter.7.cloned.1.call-start = ((), (), s32[]{:S(2)}) async-start(), calls=%async_computation.14 | async-start | bytes 1253376 | tf_op jit(solution)/shard_map/reduce_scatter | solution.py:307
  344.2 678.3 %reduce-scatter.17.cloned.1.call-start = ((), (), s32[]{:S(2)}) async-start(), calls=%async_computation.19 | async-start | bytes 5013504 | tf_op jit(solution)/shard_map/reduce_scatter | solution.py:314
  352.3 812.1 %reduce-scatter.15.cloned.1.call-start = ((), (), s32[]{:S(2)}) async-start(), calls=%async_computation.18 | async-start | bytes 5013504 | tf_op jit(solution)/shard_map/reduce_scatter | solution.py:310
  381.2 52.1 %copy-start.17 = (bf16[1024,768]{1,0:T(8,128)(2,1)S(1)}, bf16[1024,768]{1,0:T(8,128)(2,1)}, u32[]{:S(2)}) copy-start(bf16[1024,768]{1,0:T(8,128)(2,1)} %gather_fusion.2) | copy-start | bytes 4718596
  428.9 68.3 %all-to-all-start.3 = ((bf16[16,64,768]{2,1,0:T(8,128)(2,1)}), bf16[16,64,768]{2,1,0:T(8,128)(2,1)}, u32[]{:S(2)}, u32[]{:S(2)}) async-start(bf16[16,64,768]{2,1,0:T(8,128)(2,1)} %bitcast.20), calls=%async_computation.3 | async-start | bytes 3145728 | tf_op jit(solution)/shard_map/all_to_all | solution.py:263
  497.2 672.6 %copy-start.1 = (bf16[768,1536]{1,0:T(8,128)(2,1)S(1)}, bf16[768,1536]{1,0:T(8,128)(2,1)}, u32[]{:S(2)}) copy-start(bf16[768,1536]{1,0:T(8,128)(2,1)} %param.37) | copy-start | bytes 7077892
  (53 other events, 157.6 us)
Sparse Core Ops, SparseCore 0:
  102.7 25.2 all-reduce.14
  157.1 24.3 all-reduce.16
  231.1 21.6 all-reduce.18
  330.2 24.3 all-reduce.20
  359.8 137.4 reduce-scatter.12
  502.5 122.6 reduce-scatter.10
  630.6 122.5 reduce-scatter.8
  758.5 122.6 reduce-scatter.6
  887.0 135.4 reduce-scatter.16
  1028.9 135.5 reduce-scatter.14
where the time goes:
time: 1190 us; the launch traced here: 1180 us
  waiting for transfers between devices  748 us (63%)
  blocking collectives  140 us (12%)
  matrix products  131 us (11%)
  local copies, waits for them, and re-layouts  71.9 us (6%)
  other arithmetic  55.6 us (5%)
  between operations  15.4 us (1%)
  starting transfers between devices  13.6 us (1%)
    reduce_scatter x1, waiting for transfers between devices, local(): lax.psum_scatter(up_weight_grad, 'dp', scatter_dimension=0, tiled=True)  142 us
    reduce_scatter x1, waiting for transfers between devices, local(): lax.psum_scatter(down_weight_grad, 'dp', scatter_dimension=1, tiled=True)  141 us
    reduce_scatter x1, waiting for transfers between devices, local(): lax.psum_scatter(query_weight_grad, 'dp', scatter_dimension=0, tiled=True)  128 us
    reduce_scatter x1, waiting for transfers between devices, local(): lax.psum_scatter(key_weight_grad, 'dp', scatter_dimension=0, tiled=True)  128 us
    reduce_scatter x1, waiting for transfers between devices, local(): lax.psum_scatter(value_weight_grad, 'dp', scatter_dimension=0, tiled=True)  128 us
    all_to_all x1, blocking collectives, local(): lax.all_to_all(back_out, 'dp', split_axis=0, concat_axis=0, tiled=True)  47.7 us
    unnamed x1, blocking collectives  47.5 us
    psum x4, waiting for transfers between devices, combine_heads(): return lax.psum(part_sum, 'tensor')  46.9 us
  transfers between devices with their start and end apart: 12, of which 9 were waited for; matrix products, arithmetic and copies ran while one was open for 6% of the time, Pallas kernels for 0%

commit v1 on v0

v1 whole, which is shorter than its diff:
```python
import jax
import jax.numpy as jnp
from jax import lax
from jax.sharding import PartitionSpec as P

HD = 64


EPSILON = 1e-12
MASKED = -1e30
F32 = jnp.float32
BF16 = jnp.bfloat16
SWAP = [(0, 1), (1, 0)]


def product(first_op, second_op):
    return jnp.dot(first_op, second_op, preferred_element_type=F32)


def contract_rows(first_op, second_op):
    return lax.dot_general(
        first_op, second_op, (((0,), (0,)), ((), ())), preferred_element_type=F32
    )


def contract_cols(first_op, second_op):
    return lax.dot_general(
        first_op, second_op, (((1,), (1,)), ((), ())), preferred_element_type=F32
    )


def gelu_slope(values):
    cumulative = 0.5 * (1.0 + lax.erf(values * 0.7071067811865476))
    density = jnp.exp(-0.5 * values * values) * 0.3989422804014327
    return cumulative + values * density


def norm_forward(values, gain, shift):
    centre = values - jnp.mean(values, axis=-1, keepdims=True)
    inv_scale = lax.rsqrt(jnp.mean(centre * centre, axis=-1, keepdims=True) + EPSILON)
    normed = centre * inv_scale
    return (normed * gain + shift, normed, inv_scale)


def norm_backward(upstream, normed, inv_scale, gain):
    scaled = upstream * gain
    return inv_scale * (
        scaled
        - jnp.mean(scaled, axis=-1, keepdims=True)
        - normed * jnp.mean(scaled * normed, axis=-1, keepdims=True)
    )


def swap(values):
    return lax.ppermute(values, "tensor", SWAP)


def masked_scores(query_block, key_rows, segment_block, segment, score_scale):
    scores = (
        jnp.einsum("qhd,khd->hqk", query_block, key_rows, preferred_element_type=F32)
        * score_scale
    )
    return jnp.where(segment_block[None, :, None] == segment[None, None, :], scores, MASKED)


def attention_forward(query_rows, key_rows, value_rows, segment):
    row_count, head_count, head_size = query_rows.shape
    score_scale = head_size ** (-0.5)
    block_rows = min(512, row_count)
    block_count = row_count // block_rows

    def one_block(pieces):
        query_block, segment_block = pieces
        scores = masked_scores(query_block, key_rows, segment_block, segment, score_scale)
        row_peak = jnp.max(scores, axis=-1, keepdims=True)
        exp_scores = jnp.exp(scores - row_peak)
        row_total = jnp.sum(exp_scores, axis=-1, keepdims=True)
        weights = (exp_scores / row_total).astype(BF16)
        mixed_block = jnp.einsum("hqk,khd->qhd", weights, value_rows, preferred_element_type=F32)
        return (mixed_block.astype(BF16), (row_peak + jnp.log(row_total))[..., 0])

    mixed_heads, logsum = lax.map(
        one_block,
        (
            query_rows.reshape(block_count, block_rows, head_count, head_size),
            segment.reshape(block_count, block_rows),
        ),
    )
    return (mixed_heads.reshape(row_count, head_count * head_size), logsum)


def attention_backward(query_rows, key_rows, value_rows, segment, logsum, mixed_grad):
    row_count, head_count, head_size = query_rows.shape
    score_scale = head_size ** (-0.5)
    block_rows = min(512, row_count)
    block_count = row_count // block_rows

    def one_block(totals_pair, pieces):
        key_total, value_total = totals_pair
        query_block, segment_block, logsum_block, grad_block = pieces
        scores = masked_scores(query_block, key_rows, segment_block, segment, score_scale)
        softmax_rows = jnp.exp(scores - logsum_block[..., None])
        weights = softmax_rows.astype(BF16)
        value_total = value_total + jnp.einsum(
            "hqk,qhd->khd", weights, grad_block, preferred_element_type=F32
        )
        pulled = jnp.einsum("qhd,khd->hqk", grad_block, value_rows, preferred_element_type=F32)
        centred = jnp.sum(softmax_rows * pulled, axis=-1, keepdims=True)
        slopes = (softmax_rows * (pulled - centred)).astype(BF16)
        query_part = (
            jnp.einsum("hqk,khd->qhd", slopes, key_rows, preferred_element_type=F32) * score_scale
        )
        key_total = (
            key_total
            + jnp.einsum("hqk,qhd->khd", slopes, query_block, preferred_element_type=F32)
            * score_scale
        )
        return ((key_total, value_total), query_part.astype(BF16))

    zero_rows = jnp.zeros((row_count, head_count, head_size), F32)
    (key_total, value_total), query_grad = lax.scan(
        one_block,
        (zero_rows, zero_rows),
        (
            query_rows.reshape(block_count, block_rows, head_count, head_size),
            segment.reshape(block_count, block_rows),
            logsum,
            mixed_grad.reshape(block_count, block_rows, head_count, head_size),
        ),
    )
    flat_width = head_count * head_size
    return (
        query_grad.reshape(row_count, flat_width),
        key_total.astype(BF16).reshape(row_count, flat_width),
        value_total.astype(BF16).reshape(row_count, flat_width),
    )


def near_groups(groups):
    near = 4 if groups % 4 == 0 else 1
    return near, groups // near


def scatter_sum(terms):
    groups = lax.axis_size("dp")
    near, far = near_groups(groups)
    rows, columns = terms.shape
    share = rows // groups
    terms = terms.reshape(far, near, share, columns).transpose(1, 0, 2, 3)
    terms = terms.reshape(rows, columns).astype(BF16)
    within = [[f * near + n for n in range(near)] for f in range(far)]
    across = [[f * near + n for f in range(far)] for n in range(near)]
    terms = lax.psum_scatter(
        terms, "dp", scatter_dimension=0, tiled=True, axis_index_groups=within
    )
    return lax.psum_scatter(
        terms, "dp", scatter_dimension=0, tiled=True, axis_index_groups=across
    )


def local(
    tokens,
    token_slot,
    seq_lengths,
    query_weight,
    query_bias,
    key_weight,
    value_weight,
    value_bias,
    out_weight,
    out_bias,
    first_gain,
    first_shift,
    up_weight,
    up_bias,
    down_weight,
    down_bias,
    second_gain,
    second_shift,
    cotangent,
):
    groups = lax.axis_size("dp")
    row_count, feature_count = tokens.shape
    run_rows = row_count // groups
    half_run = run_rows // 2
    half = row_count // 2
    mine = lax.axis_index("tensor")

    def deal(values):
        part = lax.dynamic_slice_in_dim(
            values.reshape(groups, run_rows, feature_count), mine * half_run, half_run, 1
        )
        part = lax.all_to_all(part, "dp", split_axis=0, concat_axis=0, tiled=True)
        return part.reshape(half, feature_count)

    slots = token_slot[0]
    slots = jnp.where(mine == 0, slots, jnp.concatenate([slots[half:], slots[:half]]))
    run, place = slots // run_rows, slots % run_rows
    held = (place // half_run + mine) % 2
    column = held * half + run * half_run + place % half_run
    pick = (column[:, None] == jnp.arange(row_count, dtype=jnp.int32)[None, :]).astype(BF16)
    place_mine = (column[:, None] == jnp.arange(half, dtype=jnp.int32)[None, :]).astype(BF16)

    key_other, query_other, value_other = swap(key_weight), swap(query_weight), swap(value_weight)
    out_other, up_other, down_other = swap(out_weight), swap(up_weight), swap(down_weight)
    up_bias_other = swap(up_bias)

    token_rows = deal(tokens)
    token_rows = jnp.concatenate([token_rows, swap(token_rows)], axis=0)
    cot_rows = deal(cotangent)
    cot_rows = jnp.concatenate([cot_rows, swap(cot_rows)], axis=0)
    inputs = product(pick, token_rows).astype(BF16)
    upstream = product(pick[:half], cot_rows)

    positions = (jnp.arange(row_count, dtype=jnp.int32) + mine * half) % row_count
    ends = jnp.cumsum(seq_lengths[0])
    segment = jnp.sum((positions[:, None] >= ends[None, :]).astype(jnp.int32), axis=1)
    local_heads = query_weight.shape[1] // HD
    query_rows = (
        (product(inputs, query_weight) + query_bias)
        .astype(BF16)
        .reshape(row_count, local_heads, HD)
    )
    key_rows = product(inputs, key_weight).astype(BF16).reshape(row_count, local_heads, HD)
    value_rows = (
        (product(inputs, value_weight) + value_bias)
        .astype(BF16)
        .reshape(row_count, local_heads, HD)
    )
    mixed_flat, logsum = attention_forward(query_rows, key_rows, value_rows, segment)
    mixed_mine, mixed_other = mixed_flat[:half], swap(mixed_flat[half:])
    attended = product(mixed_mine, out_weight) + product(mixed_other, out_other)
    first_in = inputs[:half].astype(F32) + attended + out_bias
    hidden, first_normed, first_inv = norm_forward(first_in, first_gain, first_shift)
    hidden_low = hidden.astype(BF16)
    inner_mine = product(hidden_low, up_weight) + up_bias
    inner_other = product(hidden_low, up_other) + up_bias_other
    act_mine = jax.nn.gelu(inner_mine, approximate=False).astype(BF16)
    act_other = jax.nn.gelu(inner_other, approximate=False).astype(BF16)
    branch = product(act_mine, down_weight) + product(act_other, down_other)
    second_in = hidden + branch + down_bias
    output, second_normed, second_inv = norm_forward(second_in, second_gain, second_shift)
    output_low = output.astype(BF16)

    def give_back(values, extra=None):
        rows = jnp.concatenate([values, swap(values)], axis=0)
        part = contract_rows(place_mine, rows).astype(BF16)
        part = part.reshape(groups, half_run, feature_count)
        if extra is not None:
            part = jnp.concatenate([part, extra], axis=1)
        part = lax.all_to_all(part, "dp", split_axis=0, concat_axis=0, tiled=True)
        if extra is not None:
            part, extra = part[:, :half_run], part[:, half_run:]
        other = swap(part)
        low = jnp.where(mine == 0, part, other)
        high = jnp.where(mine == 0, other, part)
        whole = jnp.concatenate([low, high], axis=1).reshape(row_count, feature_count)
        return whole if extra is None else (whole, extra)

    layer_out = give_back(output_low)
    second_grad = norm_backward(upstream, second_normed, second_inv, second_gain)
    second_gain_grad = jnp.sum(upstream * second_normed, axis=0)
    second_shift_grad = jnp.sum(upstream, axis=0)
    down_bias_grad = jnp.sum(second_grad, axis=0)
    second_low = second_grad.astype(BF16)
    down_grad_mine = contract_rows(second_low, act_mine)
    down_grad_other = contract_rows(second_low, act_other)
    inner_grad_mine = (contract_cols(second_low, down_weight) * gelu_slope(inner_mine)).astype(BF16)
    inner_grad_other = (contract_cols(second_low, down_other) * gelu_slope(inner_other)).astype(
        BF16
    )
    up_bias_mine = jnp.sum(inner_grad_mine, axis=0, dtype=F32)
    up_bias_theirs = jnp.sum(inner_grad_other, axis=0, dtype=F32)
    up_grad_mine = contract_rows(hidden_low, inner_grad_mine)
    up_grad_other = contract_rows(hidden_low, inner_grad_other)
    down_sum = scatter_sum(down_grad_mine + swap(down_grad_other.astype(BF16)).astype(F32))
    up_sum = scatter_sum(up_grad_mine + swap(up_grad_other.astype(BF16)).astype(F32))

    hidden_grad = (
        second_grad
        + contract_cols(inner_grad_mine, up_weight)
        + contract_cols(inner_grad_other, up_other)
    )
    first_grad = norm_backward(hidden_grad, first_normed, first_inv, first_gain)
    first_gain_grad = jnp.sum(hidden_grad * first_normed, axis=0)
    first_shift_grad = jnp.sum(hidden_grad, axis=0)
    out_bias_grad = jnp.sum(first_grad, axis=0)
    first_low = first_grad.astype(BF16)
    out_grad_mine = contract_rows(first_low, mixed_mine)
    out_grad_other = contract_rows(first_low, mixed_other).astype(BF16)
    out_grad = out_grad_mine + swap(out_grad_other).astype(F32)
    mixed_grad_mine = contract_cols(first_low, out_weight).astype(BF16)
    mixed_grad_other = swap(contract_cols(first_low, out_other).astype(BF16))
    mixed_grad = jnp.concatenate([mixed_grad_mine, mixed_grad_other], axis=0)
    query_grad, key_grad, value_grad = attention_backward(
        query_rows,
        key_rows,
        value_rows,
        segment,
        logsum,
        mixed_grad.reshape(row_count, local_heads, HD),
    )
    query_bias_grad = jnp.sum(query_grad, axis=0, dtype=F32)
    value_bias_grad = jnp.sum(value_grad, axis=0, dtype=F32)
    query_weight_grad = contract_rows(inputs, query_grad)
    key_weight_grad = contract_rows(inputs, key_grad)
    value_weight_grad = contract_rows(inputs, value_grad)
    qkv_sum = jnp.concatenate(
        [out_grad, query_weight_grad, key_weight_grad, value_weight_grad], axis=1
    )
    qkv_sum = scatter_sum(qkv_sum).astype(F32)

    input_part = (
        contract_cols(query_grad[:half], query_weight)
        + contract_cols(key_grad[:half], key_weight)
        + contract_cols(value_grad[:half], value_weight)
        + contract_cols(swap(query_grad[half:]), query_other)
        + contract_cols(swap(key_grad[half:]), key_other)
        + contract_cols(swap(value_grad[half:]), value_other)
    )

    def padded(values):
        return lax.dynamic_update_slice_in_dim(
            jnp.zeros((2 * values.shape[0],), F32), values, mine * values.shape[0], 0
        )

    up_bias_both = padded(up_bias_mine) + lax.dynamic_update_slice_in_dim(
        jnp.zeros((2 * up_bias.shape[0],), F32), up_bias_theirs, (1 - mine) * up_bias.shape[0], 0
    )
    wide = [
        padded(query_bias_grad),
        padded(value_bias_grad),
        out_bias_grad,
        first_gain_grad,
        first_shift_grad,
        down_bias_grad,
        second_gain_grad,
        second_shift_grad,
        up_bias_both,
    ]
    terms = jnp.concatenate([v.reshape(groups, 2, -1) for v in wide], axis=2)
    pieces, rest = [], terms
    for _ in range(3):
        pieces.append(rest.astype(BF16))
        rest = rest - pieces[-1].astype(F32)
    pieces = jnp.stack(pieces, axis=1).reshape(groups, -1)
    extra_rows = -(-pieces.shape[1] // (8 * feature_count)) * 8
    pieces = jnp.pad(pieces, ((0, 0), (0, extra_rows * feature_count - pieces.shape[1])))
    input_gradient, pieces = give_back(
        (first_grad + input_part).astype(BF16),
        pieces.reshape(groups, extra_rows, feature_count),
    )
    count = terms.shape[1] * terms.shape[2]
    pieces = pieces.reshape(groups, -1)[:, : 3 * count].astype(F32)
    sums = jnp.sum(pieces, axis=0).reshape((3,) + terms.shape[1:])
    sums = sums[2] + sums[1] + sums[0]
    packed = lax.dynamic_index_in_dim(sums + swap(sums), mine, 0, keepdims=False)
    devices = 2 * groups
    small, start = [], 0
    for v in wide:
        small.append(packed[start : start + v.shape[0] // devices])
        start += v.shape[0] // devices
    (
        query_bias_sum,
        value_bias_sum,
        out_bias_sum,
        first_gain_sum,
        first_shift_sum,
        down_bias_sum,
        second_gain_sum,
        second_shift_sum,
        up_bias_sum,
    ) = small
    heads_width = query_weight.shape[1]
    return (
        layer_out,
        input_gradient,
        qkv_sum[:, heads_width : 2 * heads_width],
        query_bias_sum,
        qkv_sum[:, 2 * heads_width : 3 * heads_width],
        qkv_sum[:, 3 * heads_width :],
        value_bias_sum,
        qkv_sum[:, :heads_width].T,
        out_bias_sum,
        first_gain_sum,
        first_shift_sum,
        up_sum.astype(F32),
        up_bias_sum,
        down_sum.T.astype(F32),
        down_bias_sum,
        second_gain_sum,
        second_shift_sum,
    )


def solution(mesh):
    rows = P("dp", None)
    in_specs = (
        rows,
        rows,
        rows,
        P(None, "tensor"),
        P("tensor"),
        P(None, "tensor"),
        P(None, "tensor"),
        P("tensor"),
        P("tensor", None),
        P(),
        P(),
        P(),
        P(None, "tensor"),
        P("tensor"),
        P("tensor", None),
        P(),
        P(),
        P(),
        rows,
    )
    spread = P(("dp", "tensor"))
    out_specs = (
        rows,
        rows,
        P("dp", "tensor"),
        spread,
        P("dp", "tensor"),
        P("dp", "tensor"),
        spread,
        P("tensor", "dp"),
        spread,
        spread,
        spread,
        P("dp", "tensor"),
        spread,
        P("tensor", "dp"),
        spread,
        spread,
        spread,
    )
    return jax.shard_map(local, mesh=mesh, in_specs=in_specs, out_specs=out_specs, check_vma=False)
```

time: 1190 us -> 446 us (0.37)
  waiting for transfers between devices: 748 us -> 153 us
  blocking collectives: 140 us -> 0 us
  local copies, waits for them, and re-layouts: 71.9 us -> 35.6 us
  matrix products: 131 us -> 160 us
  starting transfers between devices: 13.6 us -> 31.6 us
  other arithmetic: 55.6 us -> 42.4 us
    reduce_scatter x6, waiting for transfers between devices: 667 us -> 118 us  [scatter_sum(): lax.psum_scatter(terms, 'dp', scatter_dimension=0, tiled=True, axis_index...]
    all_to_all x2 -> x0, blocking collectives: 92.9 us -> none  [the longest x1 47.7 us: local(): lax.all_to_all(back_out, 'dp', split_axis=0, concat_axis=0, tiled=True)]
    unnamed x1 -> x0, blocking collectives: 47.5 us -> none
    psum x4 -> x0, waiting for transfers between devices: 46.9 us -> none  [combine_heads(): return lax.psum(part_sum, 'tensor')]
    gather x4 -> x0, local copies, waits for them, and re-layouts: 23.6 us -> none  [the longest x1 7.24 us: local(): jnp.take(arrived.reshape(row_count, feature_count), slot_rows, axis=0)]
    dot_general x14 -> x19, matrix products: 65.4 us -> 86.6 us  [the longest x11 42 us: product(): return jnp.dot(first_op, second_op, preferred_element_type=F32)]
    unnamed x132 -> x108, local copies, waits for them, and re-layouts: 26.8 us -> 6.03 us
    reduce_sum x10 -> x5, other arithmetic: 22 us -> 5.27 us  [the longest x1 2.1 us: local(): down_bias_grad = jnp.sum(second_grad, axis=0)]
  transfers between devices with their start and end apart: 12 -> 32, of which waited for: 9 -> 10; matrix products, arithmetic and copies ran while one was open for 6% -> 45% of each run, Pallas kernels for 0% -> 0%
where the time goes in v1:
time: 446 us; the launch traced here: 439 us
  matrix products  160 us (36%)
  waiting for transfers between devices  153 us (34%)
  other arithmetic  42.4 us (10%)
  local copies, waits for them, and re-layouts  35.6 us (8%)
  starting transfers between devices  31.6 us (7%)
  between operations  15.7 us (4%)
    reduce_scatter x6, waiting for transfers between devices, scatter_sum(): lax.psum_scatter(terms, 'dp', scatter_dimension=0, tiled=True, axis_index...  118 us
    dot_general x11, matrix products, product(): return jnp.dot(first_op, second_op, preferred_element_type=F32)  42 us
    dot_general x12, matrix products, contract_cols(): lax.dot_general(first_op, second_op, (((1,), (1,)), ((), ())), preferred_...  32.4 us
    dot_general x11, matrix products, contract_rows(): lax.dot_general(first_op, second_op, (((0,), (0,)), ((), ())), preferred_...  20 us
    all_to_all x2, waiting for transfers between devices, deal(): part = lax.all_to_all(part, 'dp', split_axis=0, concat_axis=0, tiled=True)  18.7 us
    all_to_all x2, starting transfers between devices, deal(): part = lax.all_to_all(part, 'dp', split_axis=0, concat_axis=0, tiled=True)  13.3 us
    dot_general x2, matrix products, one_block(): jnp.einsum('qhd,khd->hqk', grad_block, value_rows, preferred_element_type...  12.5 us
    dot_general x2, matrix products, one_block(): jnp.einsum('hqk,khd->qhd', slopes, key_rows, preferred_element_type=F32)  12.4 us
  transfers between devices with their start and end apart: 32, of which 10 were waited for; matrix products, arithmetic and copies ran while one was open for 45% of the time, Pallas kernels for 0%

profile of v1, /device:TPU:0, one launch (start us, length us, event | category | flops | bytes accessed | tf_op | source)
XLA Modules:
  0.0 438.8 jit_solution(17150690554809686941)
XLA Ops:
  9.6 8.3 %all-to-all-start = ((bf16[16,32,768]{2,1,0:T(8,128)(2,1)}), bf16[16,32,768]{2,1,0:T(8,128)(2,1)S(1)}, u32[]{:S(2)}, u32[]{:S(2)}) async-start(bf16[16,32,768]{2,1,0:T(8,128)(2,1)} %constant_dynamic-slice_fusion.3), calls=%async_computation | async-start | bytes 1572864 | tf_op jit(solution)/shard_map/all_to_all | solution.py:193
  19.0 18.7 %all-to-all-done = bf16[16,32,768]{2,1,0:T(8,128)(2,1)S(1)} async-done(((bf16[16,32,768]{2,1,0:T(8,128)(2,1)}), bf16[16,32,768]{2,1,0:T(8,128)(2,1)S(1)}, u32[]{:S(2)}, u32[]{:S(2)}) %all-to-all-start) | async-done | bytes 786464 | tf_op jit(solution)/shard_map/all_to_all | solution.py:193
  38.6 4.9 %all-to-all-start.2 = ((bf16[16,32,768]{2,1,0:T(8,128)(2,1)}), bf16[16,32,768]{2,1,0:T(8,128)(2,1)}, u32[]{:S(2)}, u32[]{:S(2)}) async-start(bf16[16,32,768]{2,1,0:T(8,128)(2,1)} %constant_dynamic-slice_fusion.2), calls=%async_computation.2 | async-start | bytes 1572864 | tf_op jit(solution)/shard_map/all_to_all | solution.py:193
  55.6 23.1 %while.27 = (s32[]{:T(128)}, bf16[2,512,6,64]{1,3,2,0:T(8,128)(2,1)}, f32[2,6,512]{2,1,0:T(8,128)S(1)}, s32[2,512]{1,0:T(2,128)S(1)}, s32[1024]{0:T(1024)S(1)}, ...) while((s32[]{:T(128)}, ...), condition=%wide.region_5.6_spmd, body=%wide.region_2.5_spmd.sunk | while | flops 843772928 | bytes 42326632 | solution.py:82
  62.2 5.0 %fusion.217 = bf16[2,512,6,64]{1,3,2,0:T(8,128)(2,1)} fusion(bf16[2,512,6,64]{1,3,2,0:T(8,128)(2,1)} %get-tuple-element.471, s32[]{:T(128)} %get-tuple-element.470, bf16[1024,6,64]{0,2,1:T(8,128)(2,1)S(1)} %get-tuple-element.486, f32[6,512,1024]{2,1,0:T(8,128)S(1)} %get-tuple-element.446, f32[6,512]{1,0:T(8,128)S(1)} %fusion.216, ...), kind=kOutput, calls=%fused_computation.8.clone.1 | convolution fusion | flops 418578432 | bytes 14311936 | tf_op jit(solution)/shard_map/while/body/eval_jaxpr/hqk,khd->qhd/dot_general | solution.py:79
  73.6 5.0 %fusion.217 = bf16[2,512,6,64]{1,3,2,0:T(8,128)(2,1)} fusion(bf16[2,512,6,64]{1,3,2,0:T(8,128)(2,1)} %get-tuple-element.471, s32[]{:T(128)} %get-tuple-element.470, bf16[1024,6,64]{0,2,1:T(8,128)(2,1)S(1)} %get-tuple-element.486, f32[6,512,1024]{2,1,0:T(8,128)S(1)} %get-tuple-element.446, f32[6,512]{1,0:T(8,128)S(1)} %fusion.216, ...), kind=kOutput, calls=%fused_computation.8.clone.1 | convolution fusion | flops 418578432 | bytes 14311936 | tf_op jit(solution)/shard_map/while/body/eval_jaxpr/hqk,khd->qhd/dot_general | solution.py:79
  89.9 9.4 %fusion.39 = (bf16[512,1536]{1,0:T(8,128)(2,1)S(1)}, f32[512,1536]{1,0:T(8,128)S(1)}) fusion(f32[1536]{0:T(1024)} %param.36, bf16[512,768]{1,0:T(8,128)(2,1)S(1)} %fusion.89, bf16[768,1536]{1,0:T(8,128)(2,1)S(1)} %copy-done.48), kind=kOutput, calls=%fused_computation.64 | convolution fusion | flops 1259864064 | bytes 7870464 | tf_op jit(solution)/shard_map/dot_general | solution.py:17
  100.7 10.2 %fusion.42 = (bf16[512,1536]{1,0:T(8,128)(2,1)S(1)}, f32[512,1536]{1,0:T(8,128)S(1)}) fusion(f32[1536]{0:T(1024)} %collective-permute-done.4, bf16[512,768]{1,0:T(8,128)(2,1)S(1)} %fusion.89, bf16[768,1536]{1,0:T(8,128)(2,1)} %collective-permute-done.3), kind=kOutput, calls=%fused_computation.67 | convolution fusion | flops 1259864064 | bytes 7870464 | tf_op jit(solution)/shard_map/dot_general | solution.py:17
  125.0 4.4 %convert_reduce_fusion = (f32[1536]{0:T(1024)}, bf16[512,1536]{1,0:T(8,128)(2,1)S(1)}) fusion(f32[512,1536]{1,0:T(8,128)S(1)} %get-tuple-element.326, bf16[512,768]{1,0:T(8,128)(2,1)S(1)} %convert_element_type.246, bf16[1536,768]{1,0:T(8,128)(2,1)} %collective-permute-done.5), kind=kOutput, calls=%fused_computation.76 | convolution fusion | flops 1217395200 | bytes 7870464 | tf_op jit(solution)/shard_map/dot_general | solution.py:27
  129.4 4.8 %multiply_reduce_fusion.2 = (f32[768]{0:T(1024)}, f32[512]{0:T(512)S(1)}, f32[512]{0:T(512)S(1)}, f32[768]{0:T(1024)}, f32[512,768]{1,0:T(8,128)S(1)}) fusion(f32[512,768]{1,0:T(8,128)S(1)} %get-tuple-element.322, f32[512]{0:T(512)S(1)} %add_rsqrt_fusion.1, f32[512]{0:T(512)S(1)} %broadcast_multiply_fusion.5, f32[768]{0:T(1024)S(1)} %copy-done.31, ...), kind=kOutput, calls=%fused_computation.132 | convolution fusion | flops 1212282368 | bytes 10241024 | tf_op jit(solution)/shard_map/dot_general | solution.py:27
  148.6 62.3 %while.28 = (s32[]{:T(128)}, f32[1024,6,64]{0,2,1:T(8,128)}, f32[1024,6,64]{0,2,1:T(8,128)}, bf16[2,512,6,64]{1,3,2,0:T(8,128)(2,1)}, bf16[2,512,6,64]{1,3,2,0:T...) while((s32[]{:T(128)}, f32[1024,6,64]{0,2,1:T(8,128)}, ...), condition=%wide.region_16.17_spmd.clone, body=%wide.region_14.16_spmd.clone.sunk | while | flops 2063332352 | bytes 223580016 | solution.py:121
  151.0 6.3 %multiply_reduce_fusion.10 = (f32[6,512]{1,0:T(8,128)S(1)}, f32[6,512,1024]{2,1,0:T(8,128)S(1)}) fusion(f32[6,512,1024]{2,1,0:T(8,128)S(1)} %fusion.227, f32[6,512]{1,0:T(8,128)S(1)} %dynamic-slice_bitcast_fusion.2, pred[512,1024]{1,0:T(8,128)(4,1)S(1)} %broadcast_compare_fusion.5, bf16[1024,6,64]{0,2,1:T(8,128)(2,1)} %copy-done.6, ...), kind=kOutput, calls=%fused_computation.19.clone.1 | convolution fusion | flops 418378752 | bytes 26894848 | tf_op jit(solution)/shard_map/while/body/eval_jaxpr/qhd,khd->hqk/dot_general | solution.py:107
  157.3 5.1 %multiply_convert_fusion.2 = bf16[6,512,1024]{2,1,0:T(8,128)(2,1)} fusion(f32[6,512,1024]{2,1,0:T(8,128)S(1)} %get-tuple-element.459, f32[6,512,1024]{2,1,0:T(8,128)S(1)} %fusion.227, f32[6,512]{1,0:T(8,128)S(1)} %get-tuple-element.460, f32[6,512]{1,0:T(8,128)S(1)} %dynamic-slice_bitcast_fusion.2, pred[512,1024]{1,0:T(8,128)(4,1)S(1)} %broadcast_compare_fusion.5), kind=kLoop, calls=%fused_computation.18.clone.1 | loop fusion | flops 18874368 | bytes 32006144 | tf_op jit(solution)/shard_map/while/body/eval_jaxpr/convert_element_type | solution.py:109
  162.4 5.4 %bitcast_add_fusion.4 = f32[1024,6,64]{0,2,1:T(8,128)} fusion(f32[1024,6,64]{0,2,1:T(8,128)} %get-tuple-element.502, bf16[6,512,1024]{2,1,0:T(8,128)(2,1)} %multiply_convert_fusion.2, pred[]{:T(512)S(6)} %compare.34, bf16[2,512,6,64]{1,3,2,0:T(8,128)(2,1)} %copy-done.4, s32[]{:T(128)} %get-tuple-element.501), kind=kOutput, calls=%fused_computation.25.clone.1 | convolution fusion | flops 403832832 | bytes 9830913 | tf_op jit(solution)/shard_map/while/body/eval_jaxpr/hqk,qhd->khd/dot_general | solution.py:115
  167.8 6.2 %fusion.228 = bf16[2,512,6,64]{1,3,2,0:T(8,128)(2,1)} fusion(bf16[2,512,6,64]{1,3,2,0:T(8,128)(2,1)} %get-tuple-element.504, s32[]{:T(128)} %get-tuple-element.501, bf16[6,512,1024]{2,1,0:T(8,128)(2,1)} %multiply_convert_fusion.2, bf16[1024,6,64]{0,2,1:T(8,128)(2,1)S(1)} %get-tuple-element.521), kind=kOutput, calls=%fused_computation.29.clone.1 | convolution fusion | flops 403046400 | bytes 7471616 | tf_op jit(solution)/shard_map/while/body/eval_jaxpr/hqk,khd->qhd/dot_general | solution.py:111
  174.0 4.9 %bitcast_add_fusion.5 = f32[1024,6,64]{0,2,1:T(8,128)} fusion(f32[1024,6,64]{0,2,1:T(8,128)} %get-tuple-element.503, f32[6,512,1024]{2,1,0:T(8,128)S(1)} %copy-done.3, f32[6,512]{1,0:T(8,128)S(1)} %dynamic-slice_bitcast_fusion.2, pred[512,1024]{1,0:T(8,128)(4,1)S(1)} %broadcast_compare_fusion.5, pred[]{:T(512)S(6)} %compare.34, ...), kind=kOutput, calls=%fused_computation.24.clone.1 | convolution fusion | flops 416022528 | bytes 16662533 | tf_op jit(solution)/shard_map/while/body/eval_jaxpr/hqk,qhd->khd/dot_general | solution.py:104
  181.2 6.3 %multiply_reduce_fusion.10 = (f32[6,512]{1,0:T(8,128)S(1)}, f32[6,512,1024]{2,1,0:T(8,128)S(1)}) fusion(f32[6,512,1024]{2,1,0:T(8,128)S(1)} %fusion.227, f32[6,512]{1,0:T(8,128)S(1)} %dynamic-slice_bitcast_fusion.2, pred[512,1024]{1,0:T(8,128)(4,1)S(1)} %broadcast_compare_fusion.5, bf16[1024,6,64]{0,2,1:T(8,128)(2,1)} %copy-done.6, ...), kind=kOutput, calls=%fused_computation.19.clone.1 | convolution fusion | flops 418378752 | bytes 26894848 | tf_op jit(solution)/shard_map/while/body/eval_jaxpr/qhd,khd->hqk/dot_general | solution.py:107
  187.5 5.1 %multiply_convert_fusion.2 = bf16[6,512,1024]{2,1,0:T(8,128)(2,1)} fusion(f32[6,512,1024]{2,1,0:T(8,128)S(1)} %get-tuple-element.459, f32[6,512,1024]{2,1,0:T(8,128)S(1)} %fusion.227, f32[6,512]{1,0:T(8,128)S(1)} %get-tuple-element.460, f32[6,512]{1,0:T(8,128)S(1)} %dynamic-slice_bitcast_fusion.2, pred[512,1024]{1,0:T(8,128)(4,1)S(1)} %broadcast_compare_fusion.5), kind=kLoop, calls=%fused_computation.18.clone.1 | loop fusion | flops 18874368 | bytes 32006144 | tf_op jit(solution)/shard_map/while/body/eval_jaxpr/convert_element_type | solution.py:109
  192.5 5.8 %bitcast_add_fusion.4 = f32[1024,6,64]{0,2,1:T(8,128)} fusion(f32[1024,6,64]{0,2,1:T(8,128)} %get-tuple-element.502, bf16[6,512,1024]{2,1,0:T(8,128)(2,1)} %multiply_convert_fusion.2, pred[]{:T(512)S(6)} %compare.34, bf16[2,512,6,64]{1,3,2,0:T(8,128)(2,1)} %copy-done.4, s32[]{:T(128)} %get-tuple-element.501), kind=kOutput, calls=%fused_computation.25.clone.1 | convolution fusion | flops 403832832 | bytes 9830913 | tf_op jit(solution)/shard_map/while/body/eval_jaxpr/hqk,qhd->khd/dot_general | solution.py:115
  198.4 6.2 %fusion.228 = bf16[2,512,6,64]{1,3,2,0:T(8,128)(2,1)} fusion(bf16[2,512,6,64]{1,3,2,0:T(8,128)(2,1)} %get-tuple-element.504, s32[]{:T(128)} %get-tuple-element.501, bf16[6,512,1024]{2,1,0:T(8,128)(2,1)} %multiply_convert_fusion.2, bf16[1024,6,64]{0,2,1:T(8,128)(2,1)S(1)} %get-tuple-element.521), kind=kOutput, calls=%fused_computation.29.clone.1 | convolution fusion | flops 403046400 | bytes 7471616 | tf_op jit(solution)/shard_map/while/body/eval_jaxpr/hqk,khd->qhd/dot_general | solution.py:111
  204.6 6.1 %bitcast_add_fusion.5 = f32[1024,6,64]{0,2,1:T(8,128)} fusion(f32[1024,6,64]{0,2,1:T(8,128)} %get-tuple-element.503, f32[6,512,1024]{2,1,0:T(8,128)S(1)} %copy-done.3, f32[6,512]{1,0:T(8,128)S(1)} %dynamic-slice_bitcast_fusion.2, pred[512,1024]{1,0:T(8,128)(4,1)S(1)} %broadcast_compare_fusion.5, pred[]{:T(512)S(6)} %compare.34, ...), kind=kOutput, calls=%fused_computation.24.clone.1 | convolution fusion | flops 416022528 | bytes 16662533 | tf_op jit(solution)/shard_map/while/body/eval_jaxpr/hqk,qhd->khd/dot_general | solution.py:104
  221.0 4.3 copy.71
  232.0 4.3 collective-permute-done.21
  242.7 4.3 collective-permute-done.20
  266.1 7.1 %all-to-all-start.1 = ((bf16[16,32,768]{2,1,0:T(8,128)(2,1)}), bf16[16,32,768]{2,1,0:T(8,128)(2,1)S(1)}, u32[]{:S(2)}, u32[]{:S(2)}) async-start(bf16[16,32,768]{2,1,0:T(8,128)(2,1)} %bitcast.237), calls=%async_computation.1 | async-start | bytes 1572864 | tf_op jit(solution)/shard_map/all_to_all | solution.py:251
  287.2 6.0 %all-to-all-done.1 = bf16[16,32,768]{2,1,0:T(8,128)(2,1)S(1)} async-done(((bf16[16,32,768]{2,1,0:T(8,128)(2,1)}), bf16[16,32,768]{2,1,0:T(8,128)(2,1)S(1)}, u32[]{:S(2)}, u32[]{:S(2)}) %all-to-all-start.1) | async-done | bytes 786464 | tf_op jit(solution)/shard_map/all_to_all | solution.py:251
  293.3 5.1 %all-to-all-start.3 = ((bf16[16,40,768]{2,1,0:T(8,128)(2,1)}), bf16[16,40,768]{2,1,0:T(8,128)(2,1)S(1)}, u32[]{:S(2)}, u32[]{:S(2)}) async-start(bf16[16,40,768]{2,1,0:T(8,128)(2,1)} %pad_maximum_fusion.3), calls=%async_computation.3 | async-start | bytes 1966080 | tf_op jit(solution)/shard_map/all_to_all | solution.py:251
  299.1 19.9 %reduce-scatter.15.cloned.1.call-done = bf16[192,1536]{1,0:T(8,128)(2,1)} async-done(((bf16[768,1536]{1,0:T(8,128)(2,1)}), bf16[192,1536]{1,0:T(8,128)(2,1)}) %reduce-scatter.15.cloned.1.call-update) | async-done | bytes 589840 | tf_op jit(solution)/shard_map/reduce_scatter | solution.py:153
  324.0 36.7 %reduce-scatter.11.cloned.1.call-done = bf16[192,1536]{1,0:T(8,128)(2,1)} async-done(((bf16[768,1536]{1,0:T(8,128)(2,1)}), bf16[192,1536]{1,0:T(8,128)(2,1)}) %reduce-scatter.11.cloned.1.call-update) | async-done | bytes 589840 | tf_op jit(solution)/shard_map/reduce_scatter | solution.py:153
  363.4 21.5 %reduce-scatter.9.cloned.1.call-done = bf16[48,1536]{1,0:T(8,128)(2,1)} async-done(((bf16[192,1536]{1,0:T(8,128)(2,1)}), bf16[48,1536]{1,0:T(8,128)(2,1)}) %reduce-scatter.9.cloned.1.call-update) | async-done | bytes 147472 | tf_op jit(solution)/shard_map/reduce_scatter | solution.py:156
  388.0 19.5 %reduce-scatter.17.cloned.1.call-done = bf16[48,1536]{1,0:T(8,128)(2,1)} async-done(((bf16[192,1536]{1,0:T(8,128)(2,1)}), bf16[48,1536]{1,0:T(8,128)(2,1)}) %reduce-scatter.17.cloned.1.call-update) | async-done | bytes 147472 | tf_op jit(solution)/shard_map/reduce_scatter | solution.py:156
  409.1 20.9 %reduce-scatter.13.cloned.1.call-done = bf16[48,1536]{1,0:T(8,128)(2,1)} async-done(((bf16[192,1536]{1,0:T(8,128)(2,1)}), bf16[48,1536]{1,0:T(8,128)(2,1)}) %reduce-scatter.13.cloned.1.call-update) | async-done | bytes 147472 | tf_op jit(solution)/shard_map/reduce_scatter | solution.py:156
  (329 shorter events, 144.8 us)
Async XLA Ops:
  9.6 28.1 %all-to-all-start = ((bf16[16,32,768]{2,1,0:T(8,128)(2,1)}), bf16[16,32,768]{2,1,0:T(8,128)(2,1)S(1)}, u32[]{:S(2)}, u32[]{:S(2)}) async-start(bf16[16,32,768]{2,1,0:T(8,128)(2,1)} %constant_dynamic-slice_fusion.3), calls=%async_computation | async-start | bytes 1572864 | tf_op jit(solution)/shard_map/all_to_all | solution.py:193
  17.9 67.3 %collective-permute-start.2 = (bf16[384,768]{1,0:T(8,128)(2,1)}, bf16[384,768]{1,0:T(8,128)(2,1)}, u32[]{:S(2)}, u32[]{:S(2)}) collective-permute-start(bf16[384,768]{1,0:T(8,128)(2,1)} %param.31), channel_id=1, source_target_pairs={{0,1},{1,0},{2,3},{3,2},{4,5},{5,4},{6,7},{7,6},{8,9},{9,8},{10,11... | collective-permute-start | bytes 1769480 | tf_op jit(solution)/shard_map/ppermute | solution.py:55
  18.0 82.7 %collective-permute-start.3 = (bf16[768,1536]{1,0:T(8,128)(2,1)}, bf16[768,1536]{1,0:T(8,128)(2,1)}, u32[]{:S(2)}, u32[]{:S(2)}) collective-permute-start(bf16[768,1536]{1,0:T(8,128)(2,1)} %param.35), channel_id=1, source_target_pairs={{0,1},{1,0},{2,3},{3,2},{4,5},{5,4},{6,7},{7,6},{8,9},{9,8},{10,11... | collective-permute-start | bytes 7077896 | tf_op jit(solution)/shard_map/ppermute | solution.py:55
  18.5 82.2 %collective-permute-start.4 = (f32[1536]{0:T(1024)}, f32[1536]{0:T(1024)}, u32[]{:S(2)}, u32[]{:S(2)}) collective-permute-start(f32[1536]{0:T(1024)} %param.36), channel_id=1, source_target_pairs={{0,1},{1,0},{2,3},{3,2},{4,5},{5,4},{6,7},{7,6},{8,9},{9,8},{10,11... | collective-permute-start | bytes 18440 | tf_op jit(solution)/shard_map/ppermute | solution.py:55
  18.5 92.3 %collective-permute-start.5 = (bf16[1536,768]{1,0:T(8,128)(2,1)}, bf16[1536,768]{1,0:T(8,128)(2,1)}, u32[]{:S(2)}, u32[]{:S(2)}) collective-permute-start(bf16[1536,768]{1,0:T(8,128)(2,1)} %param.37), channel_id=1, source_target_pairs={{0,1},{1,0},{2,3},{3,2},{4,5},{5,4},{6,7},{7,6},{8,9},{9,8},{10,11... | collective-permute-start | bytes 7077896 | tf_op jit(solution)/shard_map/ppermute | solution.py:55
  37.6 6.4 %collective-permute-start = (bf16[512,768]{1,0:T(8,128)(2,1)S(1)}, bf16[512,768]{1,0:T(8,128)(2,1)S(1)}, u32[]{:S(2)}, u32[]{:S(2)}) collective-permute-start(bf16[512,768]{1,0:T(8,128)(2,1)S(1)} %bitcast.238), channel_id=1, source_target_pairs={{0,1},{1,0},{2,3},{3,2},{4,5},{5,4},{6,7},{7,6},{8,9},{9,8},{10,11... | collective-permute-start | bytes 2359304 | tf_op jit(solution)/shard_map/ppermute | solution.py:55
  38.6 46.5 %all-to-all-start.2 = ((bf16[16,32,768]{2,1,0:T(8,128)(2,1)}), bf16[16,32,768]{2,1,0:T(8,128)(2,1)}, u32[]{:S(2)}, u32[]{:S(2)}) async-start(bf16[16,32,768]{2,1,0:T(8,128)(2,1)} %constant_dynamic-slice_fusion.2), calls=%async_computation.2 | async-start | bytes 1572864 | tf_op jit(solution)/shard_map/all_to_all | solution.py:193
  43.6 254.9 %reduce-scatter.7.cloned.1.call-start = ((), (), s32[]{:S(2)}) async-start(), calls=%async_computation.10 | async-start | bytes 2949120 | tf_op jit(solution)/shard_map/reduce_scatter | solution.py:153
  80.4 5.1 %collective-permute-start.1 = (bf16[512,384]{0,1:T(8,128)(2,1)S(1)}, bf16[512,384]{0,1:T(8,128)(2,1)S(1)}, u32[]{:S(2)}, u32[]{:S(2)}) collective-permute-start(bf16[512,384]{0,1:T(8,128)(2,1)S(1)} %bitcast.247), channel_id=1, source_target_pairs={{0,1},{1,0},{2,3},{3,2},{4,5},{5,4},{6,7},{7,6},{8,9},{9,8},{10,11... | collective-permute-start | bytes 1179656 | tf_op jit(solution)/shard_map/ppermute | solution.py:55
  85.2 30.0 %collective-permute-start.8 = (bf16[512,768]{1,0:T(8,128)(2,1)}, bf16[512,768]{1,0:T(8,128)(2,1)S(1)}, u32[]{:S(2)}, u32[]{:S(2)}) collective-permute-start(bf16[512,768]{1,0:T(8,128)(2,1)} %bitcast.19), channel_id=1, source_target_pairs={{0,1},{1,0},{2,3},{3,2},{4,5},{5,4},{6,7},{7,6},{8,9},{9,8},{10,11... | collective-permute-start | bytes 2359304 | tf_op jit(solution)/shard_map/ppermute | solution.py:55
  139.3 3.4 collective-permute-start.9
  140.9 76.9 %collective-permute-start.18 = (bf16[768,384]{0,1:T(8,128)(2,1)}, bf16[768,384]{0,1:T(8,128)(2,1)}, u32[]{:S(2)}, u32[]{:S(2)}) collective-permute-start(bf16[768,384]{0,1:T(8,128)(2,1)} %convolution_convert_fusion.7), channel_id=1, source_target_pairs={{0,1},{1,0},{2,3},{3,2},{4,5},{5,4},{6,7},{7,6},{8,9},{9,8},{10,11... | collective-permute-start | bytes 1769480 | tf_op jit(solution)/shard_map/ppermute | solution.py:55
  228.7 90.3 %reduce-scatter.15.cloned.1.call-start = ((), (), s32[]{:S(2)}) async-start(), calls=%async_computation.14 | async-start | bytes 2949120 | tf_op jit(solution)/shard_map/reduce_scatter | solution.py:153
  231.7 4.6 %collective-permute-start.21 = (bf16[768,1536]{1,0:T(8,128)(2,1)S(1)}, bf16[768,1536]{1,0:T(8,128)(2,1)S(1)}, u32[]{:S(2)}, u32[]{:S(2)}) collective-permute-start(bf16[768,1536]{1,0:T(8,128)(2,1)S(1)} %convolution_convert_fusion), channel_id=1, source_target_pairs={{0,1},{1,0},{2,3},{3,2},{4,5},{5,4},{6,7},{7,6},{8,9},{9,8},{10,11... | collective-permute-start | bytes 7077896 | tf_op jit(solution)/shard_map/ppermute | solution.py:55
  239.4 121.3 %reduce-scatter.11.cloned.1.call-start = ((), (), s32[]{:S(2)}) async-start(), calls=%async_computation.12 | async-start | bytes 2949120 | tf_op jit(solution)/shard_map/reduce_scatter | solution.py:153
  242.4 4.6 %collective-permute-start.20 = (bf16[768,1536]{1,0:T(8,128)(2,1)S(1)}, bf16[768,1536]{1,0:T(8,128)(2,1)S(1)}, u32[]{:S(2)}, u32[]{:S(2)}) collective-permute-start(bf16[768,1536]{1,0:T(8,128)(2,1)S(1)} %convolution_convert_fusion.1), channel_id=1, source_target_pairs={{0,1},{1,0},{2,3},{3,2},{4,5},{5,4},{6,7},{7,6},{8,9},{9,8},{10,11... | collective-permute-start | bytes 7077896 | tf_op jit(solution)/shard_map/ppermute | solution.py:55
  250.1 23.2 %collective-permute-start.13 = (bf16[768,384]{1,0:T(8,128)(2,1)}, bf16[768,384]{1,0:T(8,128)(2,1)}, u32[]{:S(2)}, u32[]{:S(2)}) collective-permute-start(bf16[768,384]{1,0:T(8,128)(2,1)} %param.28), channel_id=1, source_target_pairs={{0,1},{1,0},{2,3},{3,2},{4,5},{5,4},{6,7},{7,6},{8,9},{9,8},{10,11... | collective-permute-start | bytes 1769480 | tf_op jit(solution)/shard_map/ppermute | solution.py:55
  250.4 25.0 %collective-permute-start.11 = (bf16[768,384]{1,0:T(8,128)(2,1)}, bf16[768,384]{1,0:T(8,128)(2,1)}, u32[]{:S(2)}, u32[]{:S(2)}) collective-permute-start(bf16[768,384]{1,0:T(8,128)(2,1)} %param.26), channel_id=1, source_target_pairs={{0,1},{1,0},{2,3},{3,2},{4,5},{5,4},{6,7},{7,6},{8,9},{9,8},{10,11... | collective-permute-start | bytes 1769480 | tf_op jit(solution)/shard_map/ppermute | solution.py:55
  250.7 26.6 %collective-permute-start.15 = (bf16[768,384]{1,0:T(8,128)(2,1)}, bf16[768,384]{1,0:T(8,128)(2,1)}, u32[]{:S(2)}, u32[]{:S(2)}) collective-permute-start(bf16[768,384]{1,0:T(8,128)(2,1)} %param.29), channel_id=1, source_target_pairs={{0,1},{1,0},{2,3},{3,2},{4,5},{5,4},{6,7},{7,6},{8,9},{9,8},{10,11... | collective-permute-start | bytes 1769480 | tf_op jit(solution)/shard_map/ppermute | solution.py:55
  250.9 11.6 %collective-permute-start.6 = (bf16[512,768]{1,0:T(8,128)(2,1)}, bf16[512,768]{1,0:T(8,128)(2,1)S(1)}, u32[]{:S(2)}, u32[]{:S(2)}) collective-permute-start(bf16[512,768]{1,0:T(8,128)(2,1)} %get-tuple-element.294), channel_id=1, source_target_pairs={{0,1},{1,0},{2,3},{3,2},{4,5},{5,4},{6,7},{7,6},{8,9},{9,8},{10,11... | collective-permute-start | bytes 2359304 | tf_op jit(solution)/shard_map/ppermute | solution.py:55
  252.0 21.4 %collective-permute-start.12 = (bf16[512,384]{0,1:T(8,128)(2,1)}, bf16[512,384]{0,1:T(8,128)(2,1)}, u32[]{:S(2)}, u32[]{:S(2)}) collective-permute-start(bf16[512,384]{0,1:T(8,128)(2,1)} %bitcast.24), channel_id=1, source_target_pairs={{0,1},{1,0},{2,3},{3,2},{4,5},{5,4},{6,7},{7,6},{8,9},{9,8},{10,11... | collective-permute-start | bytes 1179656 | tf_op jit(solution)/shard_map/ppermute | solution.py:55
  262.5 12.8 %collective-permute-start.10 = (bf16[512,384]{0,1:T(8,128)(2,1)}, bf16[512,384]{0,1:T(8,128)(2,1)}, u32[]{:S(2)}, u32[]{:S(2)}) collective-permute-start(bf16[512,384]{0,1:T(8,128)(2,1)} %bitcast.23), channel_id=1, source_target_pairs={{0,1},{1,0},{2,3},{3,2},{4,5},{5,4},{6,7},{7,6},{8,9},{9,8},{10,11... | collective-permute-start | bytes 1179656 | tf_op jit(solution)/shard_map/ppermute | solution.py:55
  266.1 27.1 %all-to-all-start.1 = ((bf16[16,32,768]{2,1,0:T(8,128)(2,1)}), bf16[16,32,768]{2,1,0:T(8,128)(2,1)S(1)}, u32[]{:S(2)}, u32[]{:S(2)}) async-start(bf16[16,32,768]{2,1,0:T(8,128)(2,1)} %bitcast.237), calls=%async_computation.1 | async-start | bytes 1572864 | tf_op jit(solution)/shard_map/all_to_all | solution.py:251
  273.3 3.9 collective-permute-start.14
  280.1 3.4 collective-permute-start.16
  293.3 27.0 %all-to-all-start.3 = ((bf16[16,40,768]{2,1,0:T(8,128)(2,1)}), bf16[16,40,768]{2,1,0:T(8,128)(2,1)S(1)}, u32[]{:S(2)}, u32[]{:S(2)}) async-start(bf16[16,40,768]{2,1,0:T(8,128)(2,1)} %pad_maximum_fusion.3), calls=%async_computation.3 | async-start | bytes 1966080 | tf_op jit(solution)/shard_map/all_to_all | solution.py:251
  298.4 86.5 %reduce-scatter.9.cloned.1.call-start = ((), (), s32[]{:S(2)}) async-start(), calls=%async_computation.11 | async-start | bytes 737280 | tf_op jit(solution)/shard_map/reduce_scatter | solution.py:156
  299.0 108.4 %reduce-scatter.17.cloned.1.call-start = ((), (), s32[]{:S(2)}) async-start(), calls=%async_computation.15 | async-start | bytes 737280 | tf_op jit(solution)/shard_map/reduce_scatter | solution.py:156
  299.0 20.0 %collective-permute-start.7 = (bf16[16,32,768]{2,1,0:T(8,128)(2,1)S(1)}, bf16[16,32,768]{2,1,0:T(8,128)(2,1)}, u32[]{:S(2)}, u32[]{:S(2)}) collective-permute-start(bf16[16,32,768]{2,1,0:T(8,128)(2,1)S(1)} %all-to-all-done.1), channel_id=1, source_target_pairs={{0,1},{1,0},{2,3},{3,2},{4,5},{5,4},{6,7},{7,6},{8,9},{9,8},{10,11... | collective-permute-start | bytes 2359304 | tf_op jit(solution)/shard_map/ppermute | solution.py:55
  319.0 111.0 %reduce-scatter.13.cloned.1.call-start = ((), (), s32[]{:S(2)}) async-start(), calls=%async_computation.13 | async-start | bytes 737280 | tf_op jit(solution)/shard_map/reduce_scatter | solution.py:156
  320.5 40.3 %collective-permute-start.17 = (bf16[16,32,768]{2,1,0:T(8,128)(2,1)S(1)}, bf16[16,32,768]{2,1,0:T(8,128)(2,1)}, u32[]{:S(2)}, u32[]{:S(2)}) collective-permute-start(bf16[16,32,768]{2,1,0:T(8,128)(2,1)S(1)} %slice.227), channel_id=1, source_target_pairs={{0,1},{1,0},{2,3},{3,2},{4,5},{5,4},{6,7},{7,6},{8,9},{9,8},{10,11... | collective-permute-start | bytes 2359304 | tf_op jit(solution)/shard_map/ppermute | solution.py:55
  320.7 2.1 collective-permute-start.19
  (66 other events, 491.0 us)
Sparse Core Ops, SparseCore 0:
  228.8 38.6 reduce-scatter.6
  270.5 48.4 reduce-scatter.14
  322.0 38.6 reduce-scatter.10
  362.8 22.0 reduce-scatter.8
  387.0 20.3 reduce-scatter.16
  409.6 20.3 reduce-scatter.12
